TPU v7x, 32 devices: a whole 2x2x4 slice. The times are simulated.
32 devices in a mesh: grp: 4 (over z), shard: 8 (over y, x, core).
Axes of the slice: x: 2, y: 2, z: 4, core: 2. Of those that a mesh axis runs over, the one named last changes fastest.
Arguments:
- frames_in: float32 [128, 256, 768], P(('grp', 'shard')), may hold values from -6 to 6
- cotangent: float32 [128, 256, 768], P(('grp', 'shard')), may hold values from -6 to 6
- time_table: bfloat16 [1000, 768], P(None, 'shard'), may hold values from -6 to 6
- ada_weight: bfloat16 [768, 6912], P('shard'), may hold values from -0.21875 to 0.21875
- ada_bias: bfloat16 [6912], P('shard'), may hold values from -4 to 4
- space_qkv: bfloat16 [768, 2304], P('shard'), may hold values from -0.21875 to 0.21875
- space_out: bfloat16 [768, 768], P('shard'), may hold values from -2.5 to 2.5
- time_qkv: bfloat16 [768, 2304], P('shard'), may hold values from -0.21875 to 0.21875
- time_out: bfloat16 [768, 768], P('shard'), may hold values from -0.875 to 0.875
- up_weight: bfloat16 [768, 3072], P('shard'), may hold values from -0.21875 to 0.21875
- up_bias: bfloat16 [3072], P('shard'), may hold values from -6 to 6
- down_weight: bfloat16 [3072, 768], P('shard'), may hold values from -0.109375 to 0.109375
- down_bias: bfloat16 [768], P('shard'), may hold values from -4 to 4
- timesteps: int32 [8], P('grp'), may hold values from 0 to 999
- task_mask: int32 [8, 16], P('grp'), may hold values 0 or 1
- clip_weight: float32 [8], P('grp'), may hold values from 0.5 to 2
- frame_table: int32 [4, 32], P('grp'), may hold values from 0 to 31, each once within a row
Outputs:
- frames_out: float32 [128, 256, 768], P(('grp', 'shard'))
- grad_frames_in: float32 [128, 256, 768], P(('grp', 'shard'))
- grad_time_table: float32 [1000, 768], P(None, 'shard')
- grad_ada_weight: float32 [768, 6912], P('shard')
- grad_ada_bias: float32 [6912], P('shard')
- grad_space_qkv: float32 [768, 2304], P('shard')
- grad_space_out: float32 [768, 768], P('shard')
- grad_time_qkv: float32 [768, 2304], P('shard')
- grad_time_out: float32 [768, 768], P('shard')
- grad_up_weight: float32 [768, 3072], P('shard')
- grad_up_bias: float32 [3072], P('shard')
- grad_down_weight: float32 [3072, 768], P('shard')
- grad_down_bias: float32 [768], P('shard')
Inputs may be any that keep to these rules, and one draw needn't show every extreme that they name: `frame_table`: each row lists every frame of its group once.
All inputs are finite; a program needn't handle non-finite values. No bound on the sum of `task_mask` on one device may be relied on, other than what follows from the above.
Results may differ from a plain program's by a relative error of at most 0.014.
Values may be sent and summed in bfloat16 or wider, within the bound.
No kernel may reach another device: no remote copies, remote signals or barrier semaphores. Data moves between devices by JAX's collectives and lax.ppermute only.
A program may use at most 256 MiB of HBM per device.

v0:
```python
from functools import partial
import jax
import jax.numpy as jnp
from jax import lax
from jax.sharding import PartitionSpec as P

HEADS = 12
HEAD_DIM = 64
HIGH = lax.Precision.HIGHEST
EPSILON = 1e-06


def layer_norm(values):
    center = values - jnp.mean(values, axis=-1, keepdims=True)
    spread = jnp.mean(center * center, axis=-1, keepdims=True)
    inverse = lax.rsqrt(spread + EPSILON)
    return (center * inverse, inverse)


def norm_back(grad_normed, normed, inverse):
    first = jnp.mean(grad_normed, axis=-1, keepdims=True)
    second = jnp.mean(grad_normed * normed, axis=-1, keepdims=True)
    return inverse * (grad_normed - first - normed * second)


def split_heads(packed, width):
    shape = packed.shape[:-1] + (HEADS, HEAD_DIM)
    return (
        packed[..., :width].reshape(shape),
        packed[..., width : 2 * width].reshape(shape),
        packed[..., 2 * width :].reshape(shape),
    )


def attend_forward(packed):
    width = packed.shape[-1] // 3
    query, keys, values = split_heads(packed, width)
    scores = jnp.einsum(
        "blmhe,bkmhe->bmhlk", query, keys, preferred_element_type=jnp.float32
    ) * HEAD_DIM ** (-0.5)
    highest = jnp.max(scores, axis=-1, keepdims=True)
    logsum = highest + jnp.log(jnp.sum(jnp.exp(scores - highest), axis=-1, keepdims=True))
    probs = jnp.exp(scores - logsum).astype(jnp.bfloat16)
    mixed = jnp.einsum("bmhlk,bkmhe->blmhe", probs, values, preferred_element_type=jnp.float32)
    return (mixed.reshape(packed.shape[:-1] + (width,)).astype(jnp.bfloat16), logsum)


def attend_backward(packed, logsum, grad_mixed):
    width = packed.shape[-1] // 3
    query, keys, values = split_heads(packed, width)
    factor = HEAD_DIM ** (-0.5)
    scores = (
        jnp.einsum("blmhe,bkmhe->bmhlk", query, keys, preferred_element_type=jnp.float32) * factor
    )
    probs = jnp.exp(scores - logsum)
    grad_heads = grad_mixed.reshape(query.shape)
    grad_probs = jnp.einsum(
        "blmhe,bkmhe->bmhlk", grad_heads, values, preferred_element_type=jnp.float32
    )
    grad_values = jnp.einsum(
        "bmhlk,blmhe->bkmhe",
        probs.astype(jnp.bfloat16),
        grad_heads,
        preferred_element_type=jnp.float32,
    )
    grad_scores = (
        probs * (grad_probs - jnp.sum(probs * grad_probs, axis=-1, keepdims=True))
    ).astype(jnp.bfloat16)
    grad_query = (
        jnp.einsum("bmhlk,bkmhe->blmhe", grad_scores, keys, preferred_element_type=jnp.float32)
        * factor
    )
    grad_keys = (
        jnp.einsum("bmhlk,blmhe->bkmhe", grad_scores, query, preferred_element_type=jnp.float32)
        * factor
    )
    shape = packed.shape[:-1] + (width,)
    joined = jnp.concatenate(
        [grad_query.reshape(shape), grad_keys.reshape(shape), grad_values.reshape(shape)], axis=-1
    )
    return joined.astype(jnp.bfloat16)


def mixer_forward(resid, shift, scale, gate, qkv_weight, out_weight):
    normed, inverse = layer_norm(resid)
    entry = (normed * (1.0 + scale) + shift).astype(jnp.bfloat16)
    packed = jnp.einsum(
        "blmd,de->blme", entry, qkv_weight, preferred_element_type=jnp.float32
    ).astype(jnp.bfloat16)
    mixed, logsum = attend_forward(packed)
    branch = jnp.einsum("blmd,de->blme", mixed, out_weight, preferred_element_type=jnp.float32)
    return (resid + gate * branch, (normed, inverse, entry, packed, logsum, mixed, branch))


def mixer_backward(grad_out, scale, gate, qkv_weight, out_weight, kept, per_clip):
    normed, inverse, entry, packed, logsum, mixed, branch = kept
    grad_gate = per_clip(grad_out * branch)
    grad_branch = (gate * grad_out).astype(jnp.bfloat16)
    grad_outw = jnp.einsum("blmd,blme->de", mixed, grad_branch, preferred_element_type=jnp.float32)
    grad_mixed = jnp.einsum(
        "blme,de->blmd", grad_branch, out_weight, preferred_element_type=jnp.float32
    ).astype(jnp.bfloat16)
    grad_packed = attend_backward(packed, logsum, grad_mixed)
    grad_qkvw = jnp.einsum("blmd,blme->de", entry, grad_packed, preferred_element_type=jnp.float32)
    grad_entry = jnp.einsum(
        "blme,de->blmd", grad_packed, qkv_weight, preferred_element_type=jnp.float32
    )
    grad_shift = per_clip(grad_entry)
    grad_scale = per_clip(grad_entry * normed)
    grad_in = grad_out + norm_back(grad_entry * (1.0 + scale), normed, inverse)
    return (grad_in, (grad_shift, grad_scale, grad_gate), grad_qkvw, grad_outw)


def feed_forward(resid, shift, scale, gate, up_full, up_bias_full, down_full, down_bias_full):
    normed, inverse = layer_norm(resid)
    entry = (normed * (1.0 + scale) + shift).astype(jnp.bfloat16)
    upward = jnp.einsum(
        "blmd,df->blmf", entry, up_full, preferred_element_type=jnp.float32
    ) + up_bias_full.astype(jnp.float32)
    active = jax.nn.gelu(upward, approximate=False).astype(jnp.bfloat16)
    downward = jnp.einsum(
        "blmf,fd->blmd", active, down_full, preferred_element_type=jnp.float32
    ) + down_bias_full.astype(jnp.float32)
    return (resid + gate * downward, (normed, inverse, entry, upward, active, downward))


def feed_backward(grad_out, scale, gate, up_full, down_full, kept, per_clip):
    normed, inverse, entry, upward, active, downward = kept
    grad_gate = per_clip(grad_out * downward)
    grad_down_in = (gate * grad_out).astype(jnp.bfloat16)
    grad_down = jnp.einsum(
        "blmf,blmd->fd", active, grad_down_in, preferred_element_type=jnp.float32
    )
    grad_down_bias = jnp.sum(grad_down_in.astype(jnp.float32), axis=(0, 1, 2))
    grad_active = jnp.einsum(
        "blmd,fd->blmf", grad_down_in, down_full, preferred_element_type=jnp.float32
    )
    _, gelu_back = jax.vjp(partial(jax.nn.gelu, approximate=False), upward)
    grad_up_in = gelu_back(grad_active)[0].astype(jnp.bfloat16)
    grad_up = jnp.einsum("blmd,blmf->df", entry, grad_up_in, preferred_element_type=jnp.float32)
    grad_up_bias = jnp.sum(grad_up_in.astype(jnp.float32), axis=(0, 1, 2))
    grad_entry = jnp.einsum(
        "blmf,df->blmd", grad_up_in, up_full, preferred_element_type=jnp.float32
    )
    grad_shift = per_clip(grad_entry)
    grad_scale = per_clip(grad_entry * normed)
    grad_in = grad_out + norm_back(grad_entry * (1.0 + scale), normed, inverse)
    return (
        grad_in,
        (grad_shift, grad_scale, grad_gate),
        grad_up,
        grad_up_bias,
        grad_down,
        grad_down_bias,
    )


def body(
    frames_in,
    cotangent,
    time_table,
    ada_weight,
    ada_bias,
    space_qkv,
    space_out,
    time_qkv,
    time_out,
    up_weight,
    up_bias,
    down_weight,
    down_bias,
    timesteps,
    task_mask,
    clip_weight,
    frame_table,
):
    shards = lax.axis_size("shard")
    shard_at = lax.axis_index("shard")
    frame_count, patches, width = frames_in.shape
    clips = timesteps.shape[0]
    frames = task_mask.shape[1]
    table = frame_table[0]
    group_frames = table.shape[0]
    columns = patches // shards
    space_qkv_full = lax.all_gather(space_qkv, "shard", axis=0, tiled=True)
    space_out_full = lax.all_gather(space_out, "shard", axis=0, tiled=True)
    time_qkv_full = lax.all_gather(time_qkv, "shard", axis=0, tiled=True)
    time_out_full = lax.all_gather(time_out, "shard", axis=0, tiled=True)
    up_full = lax.all_gather(up_weight, "shard", axis=0, tiled=True)
    down_full = lax.all_gather(down_weight, "shard", axis=0, tiled=True)
    embed = jnp.take(time_table, timesteps, axis=0).astype(jnp.float32)
    cond = jax.nn.silu(embed).astype(jnp.bfloat16)
    mod_local = jnp.dot(cond, ada_weight, preferred_element_type=jnp.float32)

    def spread(local):
        full = jnp.zeros((shards, local.shape[0]), jnp.float32)
        return lax.dynamic_update_slice_in_dim(
            full, local.astype(jnp.float32)[None], shard_at, 0
        ).reshape(-1)

    small = jnp.concatenate(
        [(mod_local + spread(ada_bias)[None]).reshape(-1), spread(up_bias), spread(down_bias)]
    )
    small = lax.psum(small, "shard")
    modul = small[: clips * 9 * width].reshape(clips, 9 * width)
    up_bias_full = small[clips * 9 * width : -width]
    down_bias_full = small[-width:]
    slot_ids = shard_at * frame_count + jnp.arange(frame_count, dtype=jnp.int32)
    frame_ids = jnp.take(table, slot_ids)
    clip_of = frame_ids // frames
    frame_of = frame_ids % frames
    clip_hot = (clip_of[:, None] == jnp.arange(clips, dtype=jnp.int32)[None, :]).astype(jnp.float32)
    frame_mod = jnp.take(modul, clip_of, axis=0)
    own_parts = [
        frame_mod[:, part_at * width : (part_at + 1) * width][:, None, None, :]
        for part_at in range(9)
    ]
    all_parts = [
        modul[:, part_at * width : (part_at + 1) * width][:, None, None, :] for part_at in range(9)
    ]
    inverse = (
        jnp.zeros((group_frames,), jnp.int32)
        .at[table]
        .set(jnp.arange(group_frames, dtype=jnp.int32))
    )

    def frame_sums(values):
        return jnp.dot(clip_hot.T, jnp.sum(values, axis=(1, 2)), precision=HIGH)

    def column_sums(values):
        return jnp.sum(values, axis=(1, 2))

    def to_columns(rows):
        parts = rows.astype(jnp.bfloat16).reshape(frame_count, shards, columns, width)
        parts = jnp.swapaxes(parts, 0, 1)
        moved = lax.all_to_all(parts, "shard", split_axis=0, concat_axis=0, tiled=True)
        return moved.reshape(group_frames, columns, width)

    def to_frames(cols):
        parts = cols.astype(jnp.bfloat16).reshape(shards, frame_count, columns, width)
        moved = lax.all_to_all(parts, "shard", split_axis=0, concat_axis=0, tiled=True)
        moved = jnp.swapaxes(moved, 0, 1)
        return moved.reshape(frame_count, patches, width).astype(jnp.float32)

    space_rows = frames_in.reshape(frame_count, patches, 1, width)
    after_space, space_kept = mixer_forward(
        space_rows, own_parts[0], own_parts[1], own_parts[2], space_qkv_full, space_out_full
    )
    received = to_columns(after_space.reshape(frame_count, patches, width))
    columned = jnp.take(received, inverse, axis=0).reshape(clips, frames, columns, width)
    columned = columned.astype(jnp.float32)
    after_time, time_kept = mixer_forward(
        columned, all_parts[3], all_parts[4], all_parts[5], time_qkv_full, time_out_full
    )
    result, mlp_kept = feed_forward(
        after_time,
        all_parts[6],
        all_parts[7],
        all_parts[8],
        up_full,
        up_bias_full,
        down_full,
        down_bias_full,
    )
    leaving = jnp.take(result.reshape(group_frames, columns, width), table, axis=0)
    frames_out = to_frames(leaving)
    row_weights = task_mask[clip_of, frame_of].astype(jnp.float32) * clip_weight[clip_of]
    weighted = cotangent * row_weights[:, None, None]
    arriving = to_columns(weighted)
    grad_result = jnp.take(arriving, inverse, axis=0).reshape(clips, frames, columns, width)
    grad_result = grad_result.astype(jnp.float32)
    grad_after_time, mlp_mods, grad_up, grad_up_bias, grad_down, grad_down_bias = feed_backward(
        grad_result, all_parts[7], all_parts[8], up_full, down_full, mlp_kept, column_sums
    )
    grad_columned, time_mods, grad_time_qkv, grad_time_out = mixer_backward(
        grad_after_time,
        all_parts[4],
        all_parts[5],
        time_qkv_full,
        time_out_full,
        time_kept,
        column_sums,
    )
    going = jnp.take(grad_columned.reshape(group_frames, columns, width), table, axis=0)
    grad_space = to_frames(going)
    grad_rows, space_mods, grad_space_qkv, grad_space_out = mixer_backward(
        grad_space.reshape(frame_count, patches, 1, width),
        own_parts[1],
        own_parts[2],
        space_qkv_full,
        space_out_full,
        space_kept,
        frame_sums,
    )
    mod_part = jnp.concatenate(space_mods + time_mods + mlp_mods, axis=1)
    small_grads = jnp.concatenate([mod_part.reshape(-1), grad_up_bias, grad_down_bias])
    small_grads = lax.psum(small_grads, "shard")
    mod_size = clips * 9 * width
    grad_modul = small_grads[:mod_size].reshape(clips, 9 * width).astype(jnp.bfloat16)
    up_dev = up_bias.shape[0]
    down_dev = down_bias.shape[0]
    bias_dev = ada_bias.shape[0]
    every_modul = lax.all_gather(grad_modul, "grp", axis=0, tiled=True)
    bias_sums = lax.psum(
        jnp.concatenate(
            [
                lax.dynamic_slice_in_dim(small_grads, mod_size + shard_at * up_dev, up_dev, 0),
                lax.dynamic_slice_in_dim(
                    small_grads, mod_size + shards * up_dev + shard_at * down_dev, down_dev, 0
                ),
            ]
        ),
        "grp",
    )
    every_embed = lax.all_gather(embed.astype(jnp.bfloat16), "grp", axis=0, tiled=True)
    every_embed = every_embed.astype(jnp.float32)
    groups = lax.axis_size("grp")
    step_slots = jnp.zeros((groups, clips), jnp.float32)
    step_slots = lax.dynamic_update_slice_in_dim(
        step_slots, timesteps.astype(jnp.float32)[None], lax.axis_index("grp"), 0
    )
    every_steps = lax.psum(step_slots.reshape(-1), "grp").astype(jnp.int32)
    every_cond = jax.nn.silu(every_embed).astype(jnp.bfloat16)
    grad_ada = jnp.einsum("cd,cj->dj", every_cond, every_modul, preferred_element_type=jnp.float32)
    grad_ada_bias = lax.dynamic_slice_in_dim(
        jnp.sum(every_modul.astype(jnp.float32), axis=0), shard_at * bias_dev, bias_dev, 0
    )
    grad_cond = jnp.einsum("cj,dj->cd", every_modul, ada_weight, preferred_element_type=jnp.float32)
    _, silu_back = jax.vjp(jax.nn.silu, every_embed)
    grad_embed = silu_back(grad_cond)[0]
    vocab = time_table.shape[0]
    onehot = (jnp.arange(vocab, dtype=jnp.int32)[:, None] == every_steps[None, :]).astype(
        jnp.float32
    )
    grad_table = jnp.dot(onehot, grad_embed, precision=HIGH)

    def total(parts):
        flat = [part.astype(jnp.bfloat16).reshape(shards, -1, width) for part in parts]
        rows = [part.shape[1] for part in flat]
        packed = jnp.concatenate(flat, axis=1)
        share = lax.psum_scatter(packed, "shard", scatter_dimension=0, tiled=True)[0]
        share = lax.psum(share, "grp").astype(jnp.float32)
        out, at = ([], 0)
        for part, count in zip(parts, rows):
            piece = share[at : at + count].reshape(part.shape[0] // shards, part.shape[1])
            out.append(piece)
            at += count
        return out

    grad_up, grad_down = total([grad_up, grad_down])
    grad_time_qkv, grad_time_out = total([grad_time_qkv, grad_time_out])
    grad_space_qkv, grad_space_out = total([grad_space_qkv, grad_space_out])
    return (
        frames_out,
        grad_rows.reshape(frame_count, patches, width),
        grad_table,
        grad_ada,
        grad_ada_bias,
        grad_space_qkv,
        grad_space_out,
        grad_time_qkv,
        grad_time_out,
        grad_up,
        bias_sums[:up_dev],
        grad_down,
        bias_sums[up_dev:],
    )


def solution(mesh):
    placed = (
        P(("grp", "shard"), None, None),
        P(("grp", "shard"), None, None),
        P(None, "shard"),
        P("shard", None),
        P("shard"),
        P("shard", None),
        P("shard", None),
        P("shard", None),
        P("shard", None),
        P("shard", None),
        P("shard"),
        P("shard", None),
        P("shard"),
        P("grp"),
        P("grp", None),
        P("grp"),
        P("grp", None),
    )
    return jax.shard_map(
        body,
        mesh=mesh,
        in_specs=placed,
        out_specs=(
            P(("grp", "shard"), None, None),
            P(("grp", "shard"), None, None),
            P(None, "shard"),
            P("shard", None),
            P("shard"),
            P("shard", None),
            P("shard", None),
            P("shard", None),
            P("shard", None),
            P("shard", None),
            P("shard"),
            P("shard", None),
            P("shard"),
        ),
        check_vma=False,
    )
```

profile of v0, /device:TPU:0, one launch (start us, length us, event | category | flops | bytes accessed | tf_op | source)
XLA Modules:
  0.0 886.2 jit_solution(1337077079453278443)
XLA Ops:
  34.7 35.1 %all-reduce.6.cloned.1.call-done = f32[17664]{0:T(1024)} async-done(((f32[17664]{0:T(1024)}), f32[17664]{0:T(1024)}) %all-reduce.6.cloned.1.call-update) | async-done | bytes 70672 | tf_op jit(solution)/shard_map/psum | solution.py:204
  71.3 35.3 %all-gather.9.cloned.1.call-done = bf16[768,2304]{1,0:T(8,128)(2,1)} async-done(((bf16[96,2304]{1,0:T(8,128)(2,1)}), bf16[768,2304]{1,0:T(8,128)(2,1)}) %all-gather.9.cloned.1.call-update) | async-done | bytes 3538960 | tf_op jit(solution)/shard_map/all_gather | solution.py:185
  106.7 7.0 fusion.9
  129.4 8.7 convolution_convert_fusion.3
  156.2 23.0 %all-to-all-done = bf16[8,4,32,768]{3,2,1,0:T(8,128)(2,1)S(1)} async-done(((bf16[8,4,32,768]{3,2,1,0:T(8,128)(2,1)}), bf16[8,4,32,768]{3,2,1,0:T(8,128)(2,1)S(1)}, u32[]{:S(2)}, u32[]{:S(2)}) %all-to-all-start) | async-done | bytes 1572896 | tf_op jit(solution)/shard_map/all_to_all | solution.py:236
  189.8 7.0 convolution_convert_fusion
  217.0 8.0 multiply_reduce_fusion.3
  255.4 11.7 %fusion.8 = (u16[2,32,3072]{2,1,0:T(8,128)(2,1)S(1)}, u16[2,32,3072]{2,1,0:T(8,128)(2,1)S(1)}, f32[2,16,32,3072]{3,2,1,0:T(8,128)S(1)}) fusion(f32[3072]{0:T(1024)S(1)} %slice.149, bf16[768,3072]{1,0:T(8,128)(2,1)} %all-gather.17.cloned.1.call-done, f32[2,16,32,768]{3,2,1,0:T(8,128)} %get-tuple-element.73, f32[2,768]{1,0:T(2,128)S(1)} %get-tuple-element.54, ...), kind=kOutput, calls=%fused_computation.51 | convolution fusion | flops 4879417344 | bytes 21266432 | tf_op jit(solution)/shard_map/blmd,df->blmf/dot_general | solution.py:117
  272.0 29.8 %multiply_convert_fusion.1 = (bf16[2,16,32,3072]{3,2,1,0:T(8,128)(2,1)}, f32[2,16,32,3072]{3,2,1,0:T(8,128)}) fusion(f32[2,16,32,3072]{3,2,1,0:T(8,128)S(1)} %get-tuple-element.75, f32[3072]{0:T(1024)S(1)} %slice.149, u16[2,32,3072]{2,1,0:T(8,128)(2,1)S(1)} %get-tuple-element.16, u16[2,32,3072]{2,1,0:T(8,128)(2,1)S(1)} %get-tuple-element.15), kind=kLoop, calls=%fused_computation.21 | loop fusion | flops 223346688 | bytes 32256000 | tf_op jit(solution)/shard_map/convert_element_type | solution.py:120
  301.7 19.7 %convert_reduce_fusion = (f32[3072]{0:T(1024)}, bf16[2,16,32,3072]{3,2,1,0:T(8,128)(2,1)}) fusion(f32[2,16,32,3072]{3,2,1,0:T(8,128)} %get-tuple-element.37, bf16[3072,768]{1,0:T(8,128)(2,1)} %all-gather.19.cloned.1.call-done, f32[2,16,32,768]{3,2,1,0:T(8,128)} %bitcast.240, f32[2,768]{1,0:T(2,128)S(1)} %get-tuple-element.55, ...), kind=kOutput, calls=%fused_computation.17 | convolution fusion | flops 4886885376 | bytes 39352320 | tf_op jit(solution)/shard_map/blmd,fd->blmf/dot_general | solution.py:135
  321.4 10.0 %multiply_reduce_fusion.5 = (f32[2,768]{1,0:T(2,128)}, f32[2,16,32]{2,1,0:T(8,128)S(1)}, f32[2,16,32]{2,1,0:T(8,128)S(1)}, f32[2,768]{1,0:T(2,128)}, f32[2,16,32,768]{3,2,1,0:T(8,128)S(1)}) fusion(f32[2,16,32,768]{3,2,1,0:T(8,128)S(1)} %copy-done.10, f32[2,16,32]{2,1,0:T(8,128)S(1)} %add_rsqrt_fusion, f32[2,16,32]{2,1,0:T(8,128)S(1)} %broadcast_multiply_fusion.4, ...), kind=kOutput, calls=%fused_computation.88 | convolution fusion | flops 4838910976 | bytes 17336320 | tf_op jit(solution)/shard_map/blmf,df->blmd/dot_general | solution.py:142
  344.2 13.1 %multiply_reduce_fusion.2 = (f32[2,32,12,16]{3,2,1,0:T(8,128)S(1)}, f32[2,32,12,16,16]{3,4,2,1,0:T(8,128)}) fusion(f32[2,32,12,16,16]{3,4,2,1,0:T(8,128)} %copy-done.5, f32[2,32,12,16]{3,2,1,0:T(8,128)} %copy-done.28, bf16[2,16,32,12,64]{4,3,2,1,0:T(8,128)(2,1)} %reshape.638, bf16[2,16,32,12,64]{4,3,2,1,0:T(8,128)(2,1)} %reshape.645), kind=kOutput, calls=%fused_computation.47 | convolution fusion | flops 25939968 | bytes 4816896 | tf_op jit(solution)/shard_map/blmhe,bkmhe->bmhlk/dot_general | solution.py:57
  413.9 6.8 reshape.657
  425.4 10.9 %multiply_reduce_fusion.7 = (f32[2,768]{1,0:T(2,128)}, f32[2,16,32]{2,1,0:T(8,128)S(1)}, f32[2,16,32]{2,1,0:T(8,128)S(1)}, f32[2,768]{1,0:T(2,128)}, f32[2,16,32,768]{3,2,1,0:T(8,128)}) fusion(f32[2,16,32,768]{3,2,1,0:T(8,128)} %bitcast.258, f32[2,16,32]{2,1,0:T(8,128)S(1)} %bitcast.274, f32[2,16,32]{2,1,0:T(8,128)S(1)} %bitcast.270, ...), kind=kOutput, calls=%fused_computation.90 | convolution fusion | flops 3630951424 | bytes 14583808 | tf_op jit(solution)/shard_map/blme,de->blmd/dot_general | solution.py:105
  436.3 9.3 %multiply_add_fusion.2 = (bf16[2,16,32,768]{3,2,1,0:T(8,128)(2,1)}, f32[2,16,32,768]{3,2,1,0:T(8,128)}) fusion(f32[2,16,32,768]{3,2,1,0:T(8,128)S(1)} %copy-done.11, f32[768]{0:T(1024)S(1)} %copy-done.61, f32[2,768]{1,0:T(2,128)S(1)} %get-tuple-element.55, bf16[2,16,32,3072]{3,2,1,0:T(8,128)(2,1)S(1)} %bitcast.250, ...), kind=kOutput, calls=%fused_computation.103 | convolution fusion | flops 4834983936 | bytes 18883584 | tf_op jit(solution)/shard_map/blmf,fd->blmd/dot_general | solution.py:121
  465.0 10.6 %bitcast_convert_fusion.1 = bf16[768,3072]{1,0:T(8,128)(2,1)} fusion(bf16[2,16,32,3072]{3,2,1,0:T(8,128)(2,1)} %get-tuple-element.86, f32[2,16,32,768]{3,2,1,0:T(8,128)} %get-tuple-element.73, f32[2,768]{1,0:T(2,128)S(1)} %copy-done.66, f32[2,768]{1,0:T(2,128)S(1)} %get-tuple-element.53, f32[2,16,32]{2,1,0:T(8,128)S(1)} %add_rsqrt_fusion, ...), kind=kOutput, calls=%fused_computation.39 | convolution fusion | flops 4838129664 | bytes 14176256 | tf_op jit(solution)/shard_map/blmd,blmf->df/dot_general | solution.py:140
  475.6 8.5 reshape.660
  484.1 8.0 all-to-all-done.3
  502.9 8.1 convolution_convert_fusion.2
  513.7 6.9 multiply_reduce_fusion
  520.6 7.6 multiply_convert_fusion
  542.8 8.8 bitcast_convert_fusion.3
  563.9 8.2 bitcast_convert_fusion
  572.1 6.9 pad_maximum_fusion
  591.2 7.0 multiply_reduce_fusion.8
  602.7 29.1 %reduce-scatter.4.cloned.1.call-done = bf16[1,384,768]{2,1,0:T(8,128)(2,1)} async-done(((bf16[8,384,768]{2,1,0:T(8,128)(2,1)}), bf16[1,384,768]{2,1,0:T(8,128)(2,1)}) %reduce-scatter.4.cloned.1.call-update) | async-done | bytes 589840 | tf_op jit(solution)/shard_map/reduce_scatter | solution.py:341
  631.8 80.2 %reduce-scatter.8.cloned.1.call-done = bf16[1,768,768]{2,1,0:T(8,128)(2,1)} async-done(((bf16[8,768,768]{2,1,0:T(8,128)(2,1)}), bf16[1,768,768]{2,1,0:T(8,128)(2,1)}) %reduce-scatter.8.cloned.1.call-update) | async-done | bytes 1179664 | tf_op jit(solution)/shard_map/reduce_scatter | solution.py:341
  712.2 10.9 %all-gather.1 = bf16[4,2,96]{2,1,0:T(2,128)(2,1)S(1)} all-gather(bf16[1,2,96]{2,1,0:T(2,128)(2,1)S(1)} %fusion.91), channel_id=1, replica_groups=mesh['grp'=4,'shard'=8] {'grp'}, dimensions={0}, use_global_device_ids=true | all-gather | bytes 1920 | tf_op jit(solution)/shard_map/all_gather | solution.py:315
  723.1 42.7 %all-reduce.8.cloned.1.call-done = f32[17664]{0:T(1024)} async-done(((f32[17664]{0:T(1024)}), f32[17664]{0:T(1024)}) %all-reduce.8.cloned.1.call-update) | async-done | bytes 70672 | tf_op jit(solution)/shard_map/psum | solution.py:297
  769.4 12.1 %all-reduce = (f32[8]{0:T(128)S(1)}, f32[480]{0:T(512)S(1)}) all-reduce(f32[8]{0:T(128)S(1)} %reshape.652, f32[480]{0:T(512)S(1)} %pad_maximum_fusion.8), channel_id=1, replica_groups=mesh['grp'=4,'shard'=8] {'grp'}, use_global_device_ids=true, to_apply=%region_20.23 | all-reduce | flops 488 | bytes 3904 | tf_op jit(solution)/shard_map/psum | solution.py:322
  782.9 14.5 %all-gather = bf16[4,2,6912]{2,1,0:T(2,128)(2,1)S(1)} all-gather(bf16[1,2,6912]{2,1,0:T(2,128)(2,1)S(1)} %reshape.753), channel_id=1, replica_groups=mesh['grp'=4,'shard'=8] {'grp'}, dimensions={0}, use_global_device_ids=true | all-gather | bytes 138240 | tf_op jit(solution)/shard_map/all_gather | solution.py:303
  801.9 64.0 %all-reduce.10.cloned.1.call-done = (bf16[384,768]{1,0:T(8,128)(2,1)}, bf16[384,768]{1,0:T(8,128)(2,1)}, bf16[768,768]{1,0:T(8,128)(2,1)}) async-done(((bf16[384,768]{1,0:T(8,128)(2,1)}, bf16[384,768]{1,0:T(8,128)(2,1)}, bf16[768,768]{1,0:T(8,128)(2,1)}), (bf16[384,768]{1,0:T(8,128)(2,1)}, bf16[384,768]{1,0:T(8,128)(2,1)}, bf16[768,768]{1,0:T(8,128)(2,1)})) %all-reduce.10.cloned.1.call-update) | async-done | bytes 2359312 | tf_op jit(solution)/shard_map/psum | solution.py:342
  (370 shorter events, 300.9 us)
Async XLA Ops:
  7.2 62.5 %all-reduce.6.cloned.1.call-start = ((), (), s32[]{:S(2)}) async-start(), calls=%async_computation.7 | async-start | bytes 147456 | tf_op jit(solution)/shard_map/psum | solution.py:204
  8.0 15.1 %copy-start.73 = (pred[2]{0:T(512)(128)(4,1)}, pred[2]{0:T(512)(128)(4,1)S(1)}, u32[]{:S(2)}) copy-start(pred[2]{0:T(512)(128)(4,1)S(1)} %compare_and_fusion.2) | copy-start | bytes 10
  15.7 91.0 %all-gather.9.cloned.1.call-start = ((), (), s32[]{:S(2)}) async-start(), calls=%async_computation.8 | async-start | bytes 3981312 | tf_op jit(solution)/shard_map/all_gather | solution.py:185
  16.5 121.6 %all-gather.11.cloned.1.call-start = ((), (), s32[]{:S(2)}) async-start(), calls=%async_computation.9 | async-start | bytes 1327104 | tf_op jit(solution)/shard_map/all_gather | solution.py:186
  17.2 172.6 %all-gather.13.cloned.1.call-start = ((), (), s32[]{:S(2)}) async-start(), calls=%async_computation.10 | async-start | bytes 3981312 | tf_op jit(solution)/shard_map/all_gather | solution.py:187
  17.8 227.1 %all-gather.15.cloned.1.call-start = ((), (), s32[]{:S(2)}) async-start(), calls=%async_computation.11 | async-start | bytes 1327104 | tf_op jit(solution)/shard_map/all_gather | solution.py:188
  18.4 237.0 %all-gather.17.cloned.1.call-start = ((), (), s32[]{:S(2)}) async-start(), calls=%async_computation.12 | async-start | bytes 5308416 | tf_op jit(solution)/shard_map/all_gather | solution.py:189
  24.4 120.8 %all-to-all-start.2 = ((bf16[8,4,32,768]{3,2,1,0:T(8,128)(2,1)}), bf16[8,4,32,768]{3,2,1,0:T(8,128)(2,1)}, u32[]{:S(2)}, u32[]{:S(2)}) async-start(bf16[8,4,32,768]{3,2,1,0:T(8,128)(2,1)} %copy.168), calls=%async_computation.2 | async-start | bytes 3145728 | tf_op jit(solution)/shard_map/all_to_all | solution.py:236
  32.3 81.4 %copy-start.56 = (f32[4,256]{1,0:T(4,128)}, f32[4,256]{1,0:T(4,128)S(1)}, u32[]{:S(2)}) copy-start(f32[4,256]{1,0:T(4,128)S(1)} %broadcast_multiply_fusion.8) | copy-start | bytes 12292
  34.7 79.1 %copy-start.59 = (f32[4,256]{1,0:T(4,128)}, f32[4,256]{1,0:T(4,128)S(1)}, u32[]{:S(2)}) copy-start(f32[4,256]{1,0:T(4,128)S(1)} %add_rsqrt_fusion.2) | copy-start | bytes 12292
  71.3 42.4 %copy-start.54 = (f32[4,768]{1,0:T(4,128)}, f32[4,768]{1,0:T(4,128)S(1)}, u32[]{:S(2)}) copy-start(f32[4,768]{1,0:T(4,128)S(1)} %get-tuple-element.52) | copy-start | bytes 36868
  71.3 42.4 %copy-start.62 = (f32[4,768]{1,0:T(4,128)}, f32[4,768]{1,0:T(4,128)S(1)}, u32[]{:S(2)}) copy-start(f32[4,768]{1,0:T(4,128)S(1)} %get-tuple-element.51) | copy-start | bytes 36868
  71.3 66.7 %copy-start.52 = (f32[4,768]{1,0:T(4,128)}, f32[4,768]{1,0:T(4,128)S(1)}, u32[]{:S(2)}) copy-start(f32[4,768]{1,0:T(4,128)S(1)} %get-tuple-element.50) | copy-start | bytes 36868
  145.2 34.0 %all-to-all-start = ((bf16[8,4,32,768]{3,2,1,0:T(8,128)(2,1)}), bf16[8,4,32,768]{3,2,1,0:T(8,128)(2,1)S(1)}, u32[]{:S(2)}, u32[]{:S(2)}) async-start(bf16[8,4,32,768]{3,2,1,0:T(8,128)(2,1)} %bitcast.226), calls=%async_computation | async-start | bytes 3145728 | tf_op jit(solution)/shard_map/all_to_all | solution.py:236
  148.8 153.0 %all-gather.19.cloned.1.call-start = ((), (), s32[]{:S(2)}) async-start(), calls=%async_computation.13 | async-start | bytes 5308416 | tf_op jit(solution)/shard_map/all_gather | solution.py:190
  149.5 453.2 %reduce-scatter.6.cloned.1.call-start = ((), (), s32[]{:S(2)}) async-start(), calls=%async_computation.16 | async-start | bytes 5308416 | tf_op jit(solution)/shard_map/reduce_scatter | solution.py:341
  152.9 102.4 %copy-start.65 = (f32[2,768]{1,0:T(2,128)}, f32[2,768]{1,0:T(2,128)S(1)}, u32[]{:S(2)}) copy-start(f32[2,768]{1,0:T(2,128)S(1)} %get-tuple-element.54) | copy-start | bytes 18436
  182.4 62.6 %copy-start.6 = (bf16[32,32,768]{2,1,0:T(8,128)(2,1)}, bf16[32,32,768]{2,1,0:T(8,128)(2,1)S(1)}, u32[]{:S(2)}) copy-start(bf16[32,32,768]{2,1,0:T(8,128)(2,1)S(1)} %gather_fusion.5) | copy-start | bytes 4718596
  301.7 19.7 %copy-start.10 = (f32[2,16,32,768]{3,2,1,0:T(8,128)S(1)}, f32[2,16,32,768]{3,2,1,0:T(8,128)}, u32[]{:S(2)}) copy-start(f32[2,16,32,768]{3,2,1,0:T(8,128)} %get-tuple-element.73) | copy-start | bytes 9437188
  338.0 19.4 %slice-start = ((s8[6291456]{0:T(1024)(128)(4,1)}), s8[2097152]{0:T(1024)(128)(4,1)S(1)}, s32[]{:S(2)}) async-start(s8[6291456]{0:T(1024)(128)(4,1)} %bitcast.230), calls=%async_computation.19 | async-start | bytes 4194304
  344.2 13.1 %slice-start.1 = ((s8[6291456]{0:T(1024)(128)(4,1)}), s8[4194304]{0:T(1024)(128)(4,1)S(1)}, s32[]{:S(2)}) async-start(s8[6291456]{0:T(1024)(128)(4,1)} %bitcast.230), calls=%async_computation.20 | async-start | bytes 8388608
  461.2 30.9 %all-to-all-start.3 = ((bf16[8,4,32,768]{3,2,1,0:T(8,128)(2,1)}), bf16[8,4,32,768]{3,2,1,0:T(8,128)(2,1)S(1)}, u32[]{:S(2)}, u32[]{:S(2)}) async-start(bf16[8,4,32,768]{3,2,1,0:T(8,128)(2,1)} %bitcast.248), calls=%async_computation.3 | async-start | bytes 3145728 | tf_op jit(solution)/shard_map/all_to_all | solution.py:241
  465.0 166.9 %reduce-scatter.4.cloned.1.call-start = ((), (), s32[]{:S(2)}) async-start(), calls=%async_computation.15 | async-start | bytes 5308416 | tf_op jit(solution)/shard_map/reduce_scatter | solution.py:341
  475.6 16.5 %copy-start.53 = (f32[4,768]{1,0:T(4,128)S(1)}, f32[4,768]{1,0:T(4,128)}, u32[]{:S(2)}) copy-start(f32[4,768]{1,0:T(4,128)} %copy-done.52) | copy-start | bytes 36868
  563.9 148.1 %reduce-scatter.8.cloned.1.call-start = ((), (), s32[]{:S(2)}) async-start(), calls=%async_computation.17 | async-start | bytes 10616832 | tf_op jit(solution)/shard_map/reduce_scatter | solution.py:341
  579.1 188.3 %all-to-all-start.1 = ((bf16[8,4,32,768]{3,2,1,0:T(8,128)(2,1)}), bf16[8,4,32,768]{3,2,1,0:T(8,128)(2,1)S(1)}, u32[]{:S(2)}, u32[]{:S(2)}) async-start(bf16[8,4,32,768]{3,2,1,0:T(8,128)(2,1)} %bitcast.32), calls=%async_computation.1 | async-start | bytes 3145728 | tf_op jit(solution)/shard_map/all_to_all | solution.py:241
  582.7 183.1 %all-reduce.8.cloned.1.call-start = ((), (), s32[]{:S(2)}) async-start(), calls=%async_computation.14 | async-start | bytes 147456 | tf_op jit(solution)/shard_map/psum | solution.py:297
  598.9 113.1 %copy-start.76 = (f32[1,2]{1,0:T(1,128)S(1)}, f32[1,2]{1,0:T(1,128)}, u32[]{:S(2)}) copy-start(f32[1,2]{1,0:T(1,128)} %get-tuple-element.59) | copy-start | bytes 28
  598.9 113.2 %copy-start.72 = (bf16[2,96]{1,0:T(2,128)(2,1)S(1)}, bf16[2,96]{1,0:T(2,128)(2,1)}, u32[]{:S(2)}) copy-start(bf16[2,96]{1,0:T(2,128)(2,1)} %copy-done.71) | copy-start | bytes 1156
  598.9 113.2 %copy-start.74 = (pred[2]{0:T(512)(128)(4,1)S(1)}, pred[2]{0:T(512)(128)(4,1)}, u32[]{:S(2)}) copy-start(pred[2]{0:T(512)(128)(4,1)} %copy-done.73) | copy-start | bytes 10
  602.7 263.3 %all-reduce.10.cloned.1.call-start = ((), (), s32[]{:S(2)}) async-start(), calls=%async_computation.18 | async-start | bytes 4718592 | tf_op jit(solution)/shard_map/psum | solution.py:342
  781.5 87.3 %copy-start.78 = (f32[480]{0:T(512)}, f32[480]{0:T(512)S(1)}, u32[]{:S(2)}) copy-start(f32[480]{0:T(512)S(1)} %get-tuple-element.32) | copy-start | bytes 5764
  (67 other events, 334.5 us)
Sparse Core Ops, SparseCore 0:
  15.8 53.8 all-reduce.5
  71.6 35.0 all-gather.8
  108.6 23.9 all-gather.10
  134.3 43.2 all-gather.12
  179.3 26.1 all-gather.14
  207.3 38.7 all-gather.16
  248.0 38.7 all-gather.18
  425.4 62.8 reduce-scatter.5
  564.0 67.7 reduce-scatter.3
  635.2 76.7 reduce-scatter.7
  715.6 50.1 all-reduce.7
  768.2 97.7 all-reduce.9
where the time goes:
time: 898 us; the launch traced here: 886 us
  waiting for transfers between devices  321 us (36%)
  matrix products  218 us (24%)
  local copies, waits for them, and re-layouts  173 us (19%)
  other arithmetic  103 us (11%)
  blocking collectives  37.5 us (4%)
  starting transfers between devices  16.7 us (2%)
  between operations  15.7 us (2%)
    reduce_scatter x3, waiting for transfers between devices, total(): lax.psum_scatter(packed, 'shard', scatter_dimension=0, tiled=True)[0]  109 us
    psum x1, waiting for transfers between devices, total(): share = lax.psum(share, 'grp').astype(jnp.float32)  64 us
    psum x1, waiting for transfers between devices, body(): small_grads = lax.psum(small_grads, 'shard')  42.7 us
    all_gather x1, waiting for transfers between devices, body(): space_qkv_full = lax.all_gather(space_qkv, 'shard', axis=0, tiled=True)  35.3 us
    psum x1, waiting for transfers between devices, body(): small = lax.psum(small, 'shard')  35.1 us
    convert_element_type x1, other arithmetic, feed_forward(): active = jax.nn.gelu(upward, approximate=False).astype(jnp.bfloat16)  29.8 us
    unnamed x176, local copies, waits for them, and re-layouts  23.9 us
    all_to_all x2, waiting for transfers between devices, to_columns(): lax.all_to_all(parts, 'shard', split_axis=0, concat_axis=0, tiled=True)  23 us
  transfers between devices with their start and end apart: 16, of which 8 were waited for; matrix products, arithmetic and copies ran while one was open for 37% of the time, Pallas kernels for 0%

commit v1 on v0

--- a/solution.py
+++ b/solution.py
@@ -294,7 +294,11 @@
     )
     mod_part = jnp.concatenate(space_mods + time_mods + mlp_mods, axis=1)
     small_grads = jnp.concatenate([mod_part.reshape(-1), grad_up_bias, grad_down_bias])
-    small_grads = lax.psum(small_grads, "shard")
+    small_grads = small_grads
+    for hop in (1, 2, 4):
+        small_grads = small_grads + lax.ppermute(
+            small_grads, "shard", [(dev, dev ^ hop) for dev in range(8)]
+        )
     mod_size = clips * 9 * width
     grad_modul = small_grads[:mod_size].reshape(clips, 9 * width).astype(jnp.bfloat16)
     up_dev = up_bias.shape[0]

time: 898 us -> 843 us (0.939)
  waiting for transfers between devices: 321 us -> 269 us
    psum x1 -> x0, waiting for transfers between devices: 42.7 us -> none  [body(): small_grads = lax.psum(small_grads, 'shard')]
    psum x1, waiting for transfers between devices: 64 us -> 51.1 us  [total(): share = lax.psum(share, 'grp').astype(jnp.float32)]
  transfers between devices with their start and end apart: 16 -> 18, of which waited for: 8 -> 8; matrix products, arithmetic and copies ran while one was open for 37% -> 40% of each run, Pallas kernels for 0% -> 0%
where the time goes in v1:
time: 843 us; the launch traced here: 831 us
  waiting for transfers between devices  269 us (32%)
  matrix products  218 us (26%)
  local copies, waits for them, and re-layouts  171 us (20%)
  other arithmetic  103 us (12%)
  blocking collectives  34.7 us (4%)
  starting transfers between devices  20.2 us (2%)
  between operations  15.4 us (2%)
    reduce_scatter x3, waiting for transfers between devices, total(): lax.psum_scatter(packed, 'shard', scatter_dimension=0, tiled=True)[0]  110 us
    psum x1, waiting for transfers between devices, total(): share = lax.psum(share, 'grp').astype(jnp.float32)  51.1 us
    all_gather x1, waiting for transfers between devices, body(): space_qkv_full = lax.all_gather(space_qkv, 'shard', axis=0, tiled=True)  35.3 us
    psum x1, waiting for transfers between devices, body(): small = lax.psum(small, 'shard')  35 us
    convert_element_type x1, other arithmetic, feed_forward(): active = jax.nn.gelu(upward, approximate=False).astype(jnp.bfloat16)  29.8 us
    unnamed x176, local copies, waits for them, and re-layouts  24 us
    all_to_all x2, waiting for transfers between devices, to_columns(): lax.all_to_all(parts, 'shard', split_axis=0, concat_axis=0, tiled=True)  23 us
    reshape x3, local copies, waits for them, and re-layouts, total(): part.astype(jnp.bfloat16).reshape(shards, -1, width)  22 us
  transfers between devices with their start and end apart: 18, of which 8 were waited for; matrix products, arithmetic and copies ran while one was open for 40% of the time, Pallas kernels for 0%

profile of v1, /device:TPU:0, one launch (start us, length us, event | category | flops | bytes accessed | tf_op | source)
XLA Modules:
  0.0 831.3 jit_solution(3027769625904227659)
XLA Ops:
  34.7 35.0 %all-reduce.5.cloned.1.call-done = f32[17664]{0:T(1024)} async-done(((f32[17664]{0:T(1024)}), f32[17664]{0:T(1024)}) %all-reduce.5.cloned.1.call-update) | async-done | bytes 70672 | tf_op jit(solution)/shard_map/psum | solution.py:204
  71.3 35.3 %all-gather.9.cloned.1.call-done = bf16[768,2304]{1,0:T(8,128)(2,1)} async-done(((bf16[96,2304]{1,0:T(8,128)(2,1)}), bf16[768,2304]{1,0:T(8,128)(2,1)}) %all-gather.9.cloned.1.call-update) | async-done | bytes 3538960 | tf_op jit(solution)/shard_map/all_gather | solution.py:185
  106.7 7.0 fusion.9
  129.4 8.7 %convolution_convert_fusion.3 = bf16[4,12,64,256]{3,2,1,0:T(8,128)(2,1)} fusion(bf16[4,256,12,64]{1,3,2,0:T(8,128)(2,1)S(1)} %bitcast.236, f32[4,12,256,256]{2,3,1,0:T(8,128)} %copy-done.3, f32[4,12,256]{2,1,0:T(8,128)S(1)} %log_add_fusion.1), kind=kOutput, calls=%fused_computation.132 | convolution fusion | flops 412876800 | bytes 15777792 | tf_op jit(solution)/shard_map/bmhlk,bkmhe->blmhe/dot_general | solution.py:44
  156.1 23.0 %all-to-all-done = bf16[8,4,32,768]{3,2,1,0:T(8,128)(2,1)S(1)} async-done(((bf16[8,4,32,768]{3,2,1,0:T(8,128)(2,1)}), bf16[8,4,32,768]{3,2,1,0:T(8,128)(2,1)S(1)}, u32[]{:S(2)}, u32[]{:S(2)}) %all-to-all-start) | async-done | bytes 1572896 | tf_op jit(solution)/shard_map/all_to_all | solution.py:236
  189.8 7.0 convolution_convert_fusion
  217.1 8.0 multiply_reduce_fusion.3
  255.4 11.6 %fusion.8 = (u16[2,32,3072]{2,1,0:T(8,128)(2,1)S(1)}, u16[2,32,3072]{2,1,0:T(8,128)(2,1)S(1)}, f32[2,16,32,3072]{3,2,1,0:T(8,128)S(1)}) fusion(f32[3072]{0:T(1024)S(1)} %slice.149, bf16[768,3072]{1,0:T(8,128)(2,1)} %all-gather.17.cloned.1.call-done, f32[2,16,32,768]{3,2,1,0:T(8,128)} %get-tuple-element.73, f32[2,768]{1,0:T(2,128)S(1)} %get-tuple-element.54, ...), kind=kOutput, calls=%fused_computation.51 | convolution fusion | flops 4879417344 | bytes 21266432 | tf_op jit(solution)/shard_map/blmd,df->blmf/dot_general | solution.py:117
  272.0 29.8 %multiply_convert_fusion.1 = (bf16[2,16,32,3072]{3,2,1,0:T(8,128)(2,1)}, f32[2,16,32,3072]{3,2,1,0:T(8,128)}) fusion(f32[2,16,32,3072]{3,2,1,0:T(8,128)S(1)} %get-tuple-element.75, f32[3072]{0:T(1024)S(1)} %slice.149, u16[2,32,3072]{2,1,0:T(8,128)(2,1)S(1)} %get-tuple-element.16, u16[2,32,3072]{2,1,0:T(8,128)(2,1)S(1)} %get-tuple-element.15), kind=kLoop, calls=%fused_computation.21 | loop fusion | flops 223346688 | bytes 32256000 | tf_op jit(solution)/shard_map/convert_element_type | solution.py:120
  301.8 19.6 %convert_reduce_fusion = (f32[3072]{0:T(1024)}, bf16[2,16,32,3072]{3,2,1,0:T(8,128)(2,1)}) fusion(f32[2,16,32,3072]{3,2,1,0:T(8,128)} %get-tuple-element.37, bf16[3072,768]{1,0:T(8,128)(2,1)} %all-gather.19.cloned.1.call-done, f32[2,16,32,768]{3,2,1,0:T(8,128)} %bitcast.240, f32[2,768]{1,0:T(2,128)S(1)} %get-tuple-element.55, ...), kind=kOutput, calls=%fused_computation.17 | convolution fusion | flops 4886885376 | bytes 39352320 | tf_op jit(solution)/shard_map/blmd,fd->blmf/dot_general | solution.py:135
  321.5 9.9 %multiply_reduce_fusion.5 = (f32[2,768]{1,0:T(2,128)}, f32[2,16,32]{2,1,0:T(8,128)S(1)}, f32[2,16,32]{2,1,0:T(8,128)S(1)}, f32[2,768]{1,0:T(2,128)}, f32[2,16,32,768]{3,2,1,0:T(8,128)S(1)}) fusion(f32[2,16,32,768]{3,2,1,0:T(8,128)S(1)} %copy-done.10, f32[2,16,32]{2,1,0:T(8,128)S(1)} %add_rsqrt_fusion, f32[2,16,32]{2,1,0:T(8,128)S(1)} %broadcast_multiply_fusion.4, ...), kind=kOutput, calls=%fused_computation.88 | convolution fusion | flops 4838910976 | bytes 17336320 | tf_op jit(solution)/shard_map/blmf,df->blmd/dot_general | solution.py:142
  344.2 13.1 %multiply_reduce_fusion.2 = (f32[2,32,12,16]{3,2,1,0:T(8,128)S(1)}, f32[2,32,12,16,16]{3,4,2,1,0:T(8,128)}) fusion(f32[2,32,12,16,16]{3,4,2,1,0:T(8,128)} %copy-done.5, f32[2,32,12,16]{3,2,1,0:T(8,128)} %copy-done.28, bf16[2,16,32,12,64]{4,3,2,1,0:T(8,128)(2,1)} %reshape.638, bf16[2,16,32,12,64]{4,3,2,1,0:T(8,128)(2,1)} %reshape.645), kind=kOutput, calls=%fused_computation.47 | convolution fusion | flops 25939968 | bytes 4816896 | tf_op jit(solution)/shard_map/blmhe,bkmhe->bmhlk/dot_general | solution.py:57
  357.4 6.7 convert_bitcast_fusion.1
  414.1 6.8 reshape.657
  425.5 10.9 %multiply_reduce_fusion.7 = (f32[2,768]{1,0:T(2,128)}, f32[2,16,32]{2,1,0:T(8,128)S(1)}, f32[2,16,32]{2,1,0:T(8,128)S(1)}, f32[2,768]{1,0:T(2,128)}, f32[2,16,32,768]{3,2,1,0:T(8,128)}) fusion(f32[2,16,32,768]{3,2,1,0:T(8,128)} %bitcast.258, f32[2,16,32]{2,1,0:T(8,128)S(1)} %bitcast.274, f32[2,16,32]{2,1,0:T(8,128)S(1)} %bitcast.270, ...), kind=kOutput, calls=%fused_computation.90 | convolution fusion | flops 3630951424 | bytes 14583808 | tf_op jit(solution)/shard_map/blme,de->blmd/dot_general | solution.py:105
  436.4 9.4 %multiply_add_fusion.2 = (bf16[2,16,32,768]{3,2,1,0:T(8,128)(2,1)}, f32[2,16,32,768]{3,2,1,0:T(8,128)}) fusion(f32[2,16,32,768]{3,2,1,0:T(8,128)S(1)} %copy-done.11, f32[768]{0:T(1024)S(1)} %copy-done.62, f32[2,768]{1,0:T(2,128)S(1)} %get-tuple-element.55, bf16[2,16,32,3072]{3,2,1,0:T(8,128)(2,1)S(1)} %bitcast.250, ...), kind=kOutput, calls=%fused_computation.103 | convolution fusion | flops 4834983936 | bytes 18883584 | tf_op jit(solution)/shard_map/blmf,fd->blmd/dot_general | solution.py:121
  465.1 10.6 %bitcast_convert_fusion.1 = bf16[768,3072]{1,0:T(8,128)(2,1)} fusion(bf16[2,16,32,3072]{3,2,1,0:T(8,128)(2,1)} %get-tuple-element.86, f32[2,16,32,768]{3,2,1,0:T(8,128)} %get-tuple-element.73, f32[2,768]{1,0:T(2,128)S(1)} %copy-done.66, f32[2,768]{1,0:T(2,128)S(1)} %get-tuple-element.53, f32[2,16,32]{2,1,0:T(8,128)S(1)} %add_rsqrt_fusion, ...), kind=kOutput, calls=%fused_computation.39 | convolution fusion | flops 4838129664 | bytes 14176256 | tf_op jit(solution)/shard_map/blmd,blmf->df/dot_general | solution.py:140
  475.7 8.5 %reshape.660 = bf16[8,384,768]{2,1,0:T(8,128)(2,1)} reshape(bf16[768,3072]{1,0:T(8,128)(2,1)} %bitcast_convert_fusion.1) | data formatting | bytes 9437184 | tf_op jit(solution)/shard_map/reshape | solution.py:342
  484.2 8.1 all-to-all-done.3
  503.0 8.1 convolution_convert_fusion.2
  513.8 6.9 multiply_reduce_fusion
  520.8 7.6 multiply_convert_fusion
  543.0 8.8 %bitcast_convert_fusion.3 = bf16[768,2304]{1,0:T(8,128)(2,1)} fusion(bf16[4,256,768]{2,1,0:T(8,128)(2,1)S(1)} %copy-done.45, bf16[4,256,768]{2,1,0:T(8,128)(2,1)} %copy.184, bf16[4,256,768]{2,1,0:T(8,128)(2,1)} %copy.183, f32[4,256,768]{2,1,0:T(8,128)} %param.21, f32[4,768]{1,0:T(4,128)S(1)} %copy-done.64, f32[4,768]{1,0:T(4,128)S(1)} %copy-done.55, ...), kind=kOutput, calls=%fused_computation.43 | convolution fusion | flops 3643736064 | bytes 11436032 | tf_op jit(solution)/shard_map/blmd,blme->de/dot_general | solution.py:104
  564.0 8.2 bitcast_convert_fusion
  572.3 6.8 pad_maximum_fusion
  591.3 7.0 multiply_reduce_fusion.8
  602.5 29.5 %reduce-scatter.4.cloned.1.call-done = bf16[1,384,768]{2,1,0:T(8,128)(2,1)} async-done(((bf16[8,384,768]{2,1,0:T(8,128)(2,1)}), bf16[1,384,768]{2,1,0:T(8,128)(2,1)}) %reduce-scatter.4.cloned.1.call-update) | async-done | bytes 589840 | tf_op jit(solution)/shard_map/reduce_scatter | solution.py:345
  631.9 80.2 %reduce-scatter.8.cloned.1.call-done = bf16[1,768,768]{2,1,0:T(8,128)(2,1)} async-done(((bf16[8,768,768]{2,1,0:T(8,128)(2,1)}), bf16[1,768,768]{2,1,0:T(8,128)(2,1)}) %reduce-scatter.8.cloned.1.call-update) | async-done | bytes 1179664 | tf_op jit(solution)/shard_map/reduce_scatter | solution.py:345
  718.4 11.4 %all-gather.1 = bf16[4,2,96]{2,1,0:T(2,128)(2,1)S(1)} all-gather(bf16[1,2,96]{2,1,0:T(2,128)(2,1)S(1)} %fusion.91), channel_id=1, replica_groups=mesh['grp'=4,'shard'=8] {'grp'}, dimensions={0}, use_global_device_ids=true | all-gather | bytes 1920 | tf_op jit(solution)/shard_map/all_gather | solution.py:319
  731.9 8.9 %all-reduce = (f32[8]{0:T(128)S(1)}, f32[480]{0:T(512)S(1)}) all-reduce(f32[8]{0:T(128)S(1)} %reshape.652, f32[480]{0:T(512)S(1)} %pad_maximum_fusion.8), channel_id=1, replica_groups=mesh['grp'=4,'shard'=8] {'grp'}, use_global_device_ids=true, to_apply=%region_20.23 | all-reduce | flops 488 | bytes 3904 | tf_op jit(solution)/shard_map/psum | solution.py:326
  741.4 14.4 %all-gather = bf16[4,2,6912]{2,1,0:T(2,128)(2,1)S(1)} all-gather(bf16[1,2,6912]{2,1,0:T(2,128)(2,1)S(1)} %reshape.753), channel_id=1, replica_groups=mesh['grp'=4,'shard'=8] {'grp'}, dimensions={0}, use_global_device_ids=true | all-gather | bytes 138240 | tf_op jit(solution)/shard_map/all_gather | solution.py:307
  760.4 51.1 %all-reduce.7.cloned.1.call-done = (bf16[384,768]{1,0:T(8,128)(2,1)}, bf16[384,768]{1,0:T(8,128)(2,1)}, bf16[768,768]{1,0:T(8,128)(2,1)}) async-done(((bf16[384,768]{1,0:T(8,128)(2,1)}, bf16[384,768]{1,0:T(8,128)(2,1)}, bf16[768,768]{1,0:T(8,128)(2,1)}), (bf16[384,768]{1,0:T(8,128)(2,1)}, bf16[384,768]{1,0:T(8,128)(2,1)}, bf16[768,768]{1,0:T(8,128)(2,1)})) %all-reduce.7.cloned.1.call-update) | async-done | bytes 2359312 | tf_op jit(solution)/shard_map/psum | solution.py:346
  (376 shorter events, 297.8 us)
Async XLA Ops:
  7.2 62.5 %all-reduce.5.cloned.1.call-start = ((), (), s32[]{:S(2)}) async-start(), calls=%async_computation.7 | async-start | bytes 147456 | tf_op jit(solution)/shard_map/psum | solution.py:204
  15.7 91.0 %all-gather.9.cloned.1.call-start = ((), (), s32[]{:S(2)}) async-start(), calls=%async_computation.8 | async-start | bytes 3981312 | tf_op jit(solution)/shard_map/all_gather | solution.py:185
  16.5 121.6 %all-gather.11.cloned.1.call-start = ((), (), s32[]{:S(2)}) async-start(), calls=%async_computation.9 | async-start | bytes 1327104 | tf_op jit(solution)/shard_map/all_gather | solution.py:186
  17.2 172.6 %all-gather.13.cloned.1.call-start = ((), (), s32[]{:S(2)}) async-start(), calls=%async_computation.10 | async-start | bytes 3981312 | tf_op jit(solution)/shard_map/all_gather | solution.py:187
  17.8 227.2 %all-gather.15.cloned.1.call-start = ((), (), s32[]{:S(2)}) async-start(), calls=%async_computation.11 | async-start | bytes 1327104 | tf_op jit(solution)/shard_map/all_gather | solution.py:188
  18.4 237.0 %all-gather.17.cloned.1.call-start = ((), (), s32[]{:S(2)}) async-start(), calls=%async_computation.12 | async-start | bytes 5308416 | tf_op jit(solution)/shard_map/all_gather | solution.py:189
  24.4 120.8 %all-to-all-start.2 = ((bf16[8,4,32,768]{3,2,1,0:T(8,128)(2,1)}), bf16[8,4,32,768]{3,2,1,0:T(8,128)(2,1)}, u32[]{:S(2)}, u32[]{:S(2)}) async-start(bf16[8,4,32,768]{3,2,1,0:T(8,128)(2,1)} %copy.168), calls=%async_computation.2 | async-start | bytes 3145728 | tf_op jit(solution)/shard_map/all_to_all | solution.py:236
  32.3 81.4 %copy-start.58 = (f32[4,256]{1,0:T(4,128)}, f32[4,256]{1,0:T(4,128)S(1)}, u32[]{:S(2)}) copy-start(f32[4,256]{1,0:T(4,128)S(1)} %broadcast_multiply_fusion.8) | copy-start | bytes 12292
  34.7 79.0 %copy-start.60 = (f32[4,256]{1,0:T(4,128)}, f32[4,256]{1,0:T(4,128)S(1)}, u32[]{:S(2)}) copy-start(f32[4,256]{1,0:T(4,128)S(1)} %add_rsqrt_fusion.2) | copy-start | bytes 12292
  71.3 42.4 %copy-start.54 = (f32[4,768]{1,0:T(4,128)}, f32[4,768]{1,0:T(4,128)S(1)}, u32[]{:S(2)}) copy-start(f32[4,768]{1,0:T(4,128)S(1)} %get-tuple-element.52) | copy-start | bytes 36868
  71.3 42.4 %copy-start.63 = (f32[4,768]{1,0:T(4,128)}, f32[4,768]{1,0:T(4,128)S(1)}, u32[]{:S(2)}) copy-start(f32[4,768]{1,0:T(4,128)S(1)} %get-tuple-element.51) | copy-start | bytes 36868
  71.3 66.7 %copy-start.52 = (f32[4,768]{1,0:T(4,128)}, f32[4,768]{1,0:T(4,128)S(1)}, u32[]{:S(2)}) copy-start(f32[4,768]{1,0:T(4,128)S(1)} %get-tuple-element.50) | copy-start | bytes 36868
  145.2 34.0 %all-to-all-start = ((bf16[8,4,32,768]{3,2,1,0:T(8,128)(2,1)}), bf16[8,4,32,768]{3,2,1,0:T(8,128)(2,1)S(1)}, u32[]{:S(2)}, u32[]{:S(2)}) async-start(bf16[8,4,32,768]{3,2,1,0:T(8,128)(2,1)} %bitcast.226), calls=%async_computation | async-start | bytes 3145728 | tf_op jit(solution)/shard_map/all_to_all | solution.py:236
  148.8 153.0 %all-gather.19.cloned.1.call-start = ((), (), s32[]{:S(2)}) async-start(), calls=%async_computation.13 | async-start | bytes 5308416 | tf_op jit(solution)/shard_map/all_gather | solution.py:190
  149.5 452.9 %reduce-scatter.6.cloned.1.call-start = ((), (), s32[]{:S(2)}) async-start(), calls=%async_computation.15 | async-start | bytes 5308416 | tf_op jit(solution)/shard_map/reduce_scatter | solution.py:345
  152.9 102.5 %copy-start.65 = (f32[2,768]{1,0:T(2,128)}, f32[2,768]{1,0:T(2,128)S(1)}, u32[]{:S(2)}) copy-start(f32[2,768]{1,0:T(2,128)S(1)} %get-tuple-element.54) | copy-start | bytes 18436
  182.4 62.6 %copy-start.6 = (bf16[32,32,768]{2,1,0:T(8,128)(2,1)}, bf16[32,32,768]{2,1,0:T(8,128)(2,1)S(1)}, u32[]{:S(2)}) copy-start(bf16[32,32,768]{2,1,0:T(8,128)(2,1)S(1)} %gather_fusion.5) | copy-start | bytes 4718596
  301.8 19.7 %copy-start.10 = (f32[2,16,32,768]{3,2,1,0:T(8,128)S(1)}, f32[2,16,32,768]{3,2,1,0:T(8,128)}, u32[]{:S(2)}) copy-start(f32[2,16,32,768]{3,2,1,0:T(8,128)} %get-tuple-element.73) | copy-start | bytes 9437188
  338.0 19.4 %slice-start = ((s8[6291456]{0:T(1024)(128)(4,1)}), s8[2097152]{0:T(1024)(128)(4,1)S(1)}, s32[]{:S(2)}) async-start(s8[6291456]{0:T(1024)(128)(4,1)} %bitcast.230), calls=%async_computation.18 | async-start | bytes 4194304
  461.3 30.9 %all-to-all-start.3 = ((bf16[8,4,32,768]{3,2,1,0:T(8,128)(2,1)}), bf16[8,4,32,768]{3,2,1,0:T(8,128)(2,1)S(1)}, u32[]{:S(2)}, u32[]{:S(2)}) async-start(bf16[8,4,32,768]{3,2,1,0:T(8,128)(2,1)} %bitcast.248), calls=%async_computation.3 | async-start | bytes 3145728 | tf_op jit(solution)/shard_map/all_to_all | solution.py:241
  465.0 166.9 %reduce-scatter.4.cloned.1.call-start = ((), (), s32[]{:S(2)}) async-start(), calls=%async_computation.14 | async-start | bytes 5308416 | tf_op jit(solution)/shard_map/reduce_scatter | solution.py:345
  475.7 16.5 %copy-start.53 = (f32[4,768]{1,0:T(4,128)S(1)}, f32[4,768]{1,0:T(4,128)}, u32[]{:S(2)}) copy-start(f32[4,768]{1,0:T(4,128)} %copy-done.52) | copy-start | bytes 36868
  564.0 148.2 %reduce-scatter.8.cloned.1.call-start = ((), (), s32[]{:S(2)}) async-start(), calls=%async_computation.16 | async-start | bytes 10616832 | tf_op jit(solution)/shard_map/reduce_scatter | solution.py:345
  579.1 150.8 %all-to-all-start.1 = ((bf16[8,4,32,768]{3,2,1,0:T(8,128)(2,1)}), bf16[8,4,32,768]{3,2,1,0:T(8,128)(2,1)S(1)}, u32[]{:S(2)}, u32[]{:S(2)}) async-start(bf16[8,4,32,768]{3,2,1,0:T(8,128)(2,1)} %bitcast.32), calls=%async_computation.1 | async-start | bytes 3145728 | tf_op jit(solution)/shard_map/all_to_all | solution.py:241
  582.7 228.8 %all-reduce.7.cloned.1.call-start = ((), (), s32[]{:S(2)}) async-start(), calls=%async_computation.17 | async-start | bytes 4718592 | tf_op jit(solution)/shard_map/psum | solution.py:346
  601.6 116.6 %copy-start.72 = (bf16[2,96]{1,0:T(2,128)(2,1)S(1)}, bf16[2,96]{1,0:T(2,128)(2,1)}, u32[]{:S(2)}) copy-start(bf16[2,96]{1,0:T(2,128)(2,1)} %copy-done.71) | copy-start | bytes 1156
  601.6 116.6 %copy-start.74 = (pred[2]{0:T(512)(128)(4,1)S(1)}, pred[2]{0:T(512)(128)(4,1)}, u32[]{:S(2)}) copy-start(pred[2]{0:T(512)(128)(4,1)} %copy-done.73) | copy-start | bytes 10
  601.6 116.7 %copy-start.76 = (f32[1,2]{1,0:T(1,128)S(1)}, f32[1,2]{1,0:T(1,128)}, u32[]{:S(2)}) copy-start(f32[1,2]{1,0:T(1,128)} %get-tuple-element.59) | copy-start | bytes 28
  602.0 110.1 %collective-permute-start = (f32[17664]{0:T(1024)S(1)}, f32[17664]{0:T(1024)S(1)}, u32[]{:S(2)}, u32[]{:S(2)}) collective-permute-start(f32[17664]{0:T(1024)S(1)} %pad_maximum_fusion.7), channel_id=1, source_target_pairs={{0,1},{1,0},{2,3},{3,2},{4,5},{5,4},{6,7},{7,6},{8,9},{9,8},{10,11... | collective-permute-start | bytes 211976 | tf_op jit(solution)/shard_map/ppermute | solution.py:299
  712.2 4.4 collective-permute-start.1
  716.6 13.1 %collective-permute-start.2 = (f32[17664]{0:T(1024)S(1)}, f32[17664]{0:T(1024)S(1)}, u32[]{:S(2)}, u32[]{:S(2)}) collective-permute-start(f32[17664]{0:T(1024)S(1)} %add.375), channel_id=1, source_target_pairs={{0,4},{1,5},{2,6},{3,7},{4,0},{5,1},{6,2},{7,3},{8,12},{9,13},{10,... | collective-permute-start | bytes 211976 | tf_op jit(solution)/shard_map/ppermute | solution.py:299
  740.8 73.4 %copy-start.78 = (f32[480]{0:T(512)}, f32[480]{0:T(512)S(1)}, u32[]{:S(2)}) copy-start(f32[480]{0:T(512)S(1)} %get-tuple-element.32) | copy-start | bytes 5764
  (69 other events, 362.6 us)
Sparse Core Ops, SparseCore 0:
  15.8 53.8 all-reduce.4
  71.6 35.0 all-gather.8
  108.6 23.9 all-gather.10
  134.3 43.2 all-gather.12
  179.3 26.2 all-gather.14
  207.3 38.7 all-gather.16
  248.0 38.8 all-gather.18
  425.5 62.8 reduce-scatter.5
  564.1 67.7 reduce-scatter.3
  635.3 76.8 reduce-scatter.7
  714.7 96.7 all-reduce.6
